TPU v7x, 32 devices: a whole 2x2x4 slice. The times are simulated.
32 devices in a mesh: tm: 8 (over z, x), pack: 4 (over y, core).
Axes of the slice: x: 2, y: 2, z: 4, core: 2. Of those that a mesh axis runs over, the one named last changes fastest.
Arguments:
- queries: bfloat16 [4, 4096, 1024], P('pack', 'tm'), may hold values from -8 to 8
- keys: bfloat16 [4, 4096, 1024], P('pack', 'tm'), may hold values from -8 to 8
- values: bfloat16 [4, 4096, 1024], P('pack', 'tm'), may hold values from -6 to 6
- w_out: bfloat16 [1024, 1024], replicated, may hold values from -0.1875 to 0.1875
- norm_gain: float32 [1024], replicated, may hold values from 0.1 to 1.9
- block_owner: int32 [4, 32, 1], P('pack', 'tm'), may hold values from 0 to 3; in each aligned block of 4 rows (0 to 3, 4 to 7, ..., all dimensions but the last counted through in order) at most 2 rows name the same one
- block_base: int32 [4, 32], P('pack', 'tm'), may hold values from 0 to 112
- frame_offset: int32 [4, 32, 128], P('pack', 'tm'), may hold values from 0 to 15, never falling along the last dimension, each value on 1 to 16 neighbouring positions
Outputs:
- encoded: bfloat16 [4, 4096, 1024], P('pack', 'tm')
- pooled: bfloat16 [4, 1024, 1024], P('pack', 'tm')
Inputs may be any that keep to these rules, and one draw needn't show every extreme that they name: `block_owner`: among the 4 blocks of one device (aligned runs of the list), at most 2 name the same owner. `frame_offset`: within each block of 128 frames the offsets never fall and each of 0 to 15 occurs.
All inputs are finite; a program needn't handle non-finite values.
Results may differ from a plain program's by a relative error of at most 0.008.
Values may be sent and summed in bfloat16 or wider, within the bound.
No kernel may reach another device: no remote copies, remote signals or barrier semaphores. Data moves between devices by JAX's collectives and lax.ppermute only.
A program may use at most 128 MiB of HBM per device.

v0:
```python
import math
import jax
import jax.numpy as jnp
from jax import lax
from jax.sharding import PartitionSpec as P

HEADS = 16
LANDMARKS = 256
BLOCK = 128
POOL_DEV = 128


def mix_heads(query_rows, mark_keys, mark_values, head_count):
    row_count, model_width = query_rows.shape
    head_dim = model_width // head_count
    query_heads = query_rows.reshape(row_count, head_count, head_dim)
    key_heads = mark_keys.reshape(-1, head_count, head_dim)
    value_heads = mark_values.reshape(-1, head_count, head_dim)
    scores = jnp.einsum(
        "nhe,mhe->nhm", query_heads, key_heads, preferred_element_type=jnp.float32
    ) * head_dim ** (-0.5)
    weights = jnp.exp(scores - jnp.max(scores, axis=-1, keepdims=True))
    totals = jnp.sum(weights, axis=-1)
    blended = jnp.einsum(
        "nhm,mhe->nhe",
        weights.astype(jnp.bfloat16),
        value_heads,
        preferred_element_type=jnp.float32,
    )
    return (blended / totals[..., None]).reshape(row_count, model_width).astype(jnp.bfloat16)


def mix_blocked(query_rows, mark_keys, mark_values, head_count):
    row_count, model_width = query_rows.shape
    row_block = math.gcd(row_count, 1024)
    stacked = query_rows.reshape(row_count // row_block, row_block, model_width)
    mixed_rows = lax.map(
        lambda frame_block: mix_heads(frame_block, mark_keys, mark_values, head_count), stacked
    )
    return mixed_rows.reshape(row_count, model_width)


def local(queries, keys, values, w_out, norm_gain, block_owner, block_base, frame_offset):
    frame_q = queries[0]
    frame_k = keys[0]
    frame_v = values[0]
    frame_count, model_width = frame_q.shape
    span = frame_count // LANDMARKS
    mark_queries = jnp.mean(
        frame_q.reshape(LANDMARKS, span, model_width), axis=1, dtype=jnp.float32
    ).astype(jnp.bfloat16)
    mark_keys = jnp.mean(
        frame_k.reshape(LANDMARKS, span, model_width), axis=1, dtype=jnp.float32
    ).astype(jnp.bfloat16)
    mark_values = mix_heads(mark_queries, frame_k, frame_v, HEADS)
    spread_q, spread_k, spread_v = (
        lax.all_to_all(frame_q, "tm", split_axis=1, concat_axis=0, tiled=True),
        lax.all_to_all(mark_keys, "tm", split_axis=1, concat_axis=0, tiled=True),
        lax.all_to_all(mark_values, "tm", split_axis=1, concat_axis=0, tiled=True),
    )
    local_heads = HEADS // lax.axis_size("tm")
    head_result = mix_blocked(spread_q, spread_k, spread_v, local_heads)
    attended = lax.all_to_all(head_result, "tm", split_axis=0, concat_axis=1, tiled=True)
    projected = jnp.dot(attended, w_out, preferred_element_type=jnp.float32)
    scaled = projected * lax.rsqrt(jnp.mean(projected * projected, axis=-1, keepdims=True) + 1e-06)
    encoded = (scaled * norm_gain).astype(jnp.bfloat16)
    pack_count = lax.axis_size("pack")
    owners = block_owner[0, :, 0]
    block_count = owners.shape[0]
    slot_count = max(2, 2 * block_count // pack_count)
    pack_range = jnp.arange(pack_count, dtype=jnp.int32)
    dest_hits = (owners[:, None] == pack_range[None, :]).astype(jnp.int32)
    slot_rank = jnp.sum((jnp.cumsum(dest_hits, axis=0) - dest_hits) * dest_hits, axis=1)
    chosen = (owners[None, None, :] == pack_range[:, None, None]) & (
        slot_rank[None, None, :] == jnp.arange(slot_count, dtype=jnp.int32)[None, :, None]
    )
    filled = jnp.any(chosen, axis=-1)
    source_block = jnp.sum(
        chosen.astype(jnp.int32) * jnp.arange(block_count, dtype=jnp.int32)[None, None, :], axis=-1
    )
    frame_blocks = encoded.reshape(block_count, BLOCK, model_width)
    offsets = frame_offset[0]
    block_bases = block_base[0]
    sent_rows = jnp.where(
        filled[..., None, None],
        jnp.take(frame_blocks, source_block, axis=0),
        jnp.zeros((), jnp.bfloat16),
    )
    row_targets = jnp.take(block_bases, source_block)[..., None] + jnp.take(
        offsets, source_block, axis=0
    )
    sent_targets = jnp.where(filled[..., None], row_targets, -1).astype(jnp.bfloat16)
    got_rows, got_targets = (
        lax.all_to_all(sent_rows, "pack", split_axis=0, concat_axis=0, tiled=True),
        lax.all_to_all(sent_targets, "pack", split_axis=0, concat_axis=0, tiled=True),
    )
    pool_rows = jnp.arange(POOL_DEV, dtype=jnp.int32).astype(jnp.bfloat16)
    placing = got_targets[:, :, None, :] == pool_rows[None, None, :, None]
    pool_sums = jnp.einsum(
        "scrf,scfd->rd", placing.astype(jnp.bfloat16), got_rows, preferred_element_type=jnp.float32
    )
    pool_counts = jnp.sum(placing.astype(jnp.float32), axis=(0, 1, 3))
    pooled = (pool_sums / jnp.maximum(pool_counts, 1.0)[:, None]).astype(jnp.bfloat16)
    return (encoded[None], pooled[None])


def solution(mesh):
    return jax.shard_map(
        local,
        mesh=mesh,
        in_specs=(
            P("pack", "tm", None),
            P("pack", "tm", None),
            P("pack", "tm", None),
            P(),
            P(),
            P("pack", "tm", None),
            P("pack", "tm"),
            P("pack", "tm", None),
        ),
        out_specs=(P("pack", "tm", None), P("pack", "tm", None)),
        check_vma=False,
    )
```

profile of v0, /device:TPU:0, one launch (start us, length us, event | category | flops | bytes accessed | tf_op | source)
XLA Modules:
  0.0 267.6 jit_solution(12814046430353551243)
XLA Ops:
  0.7 3.6 %reshape.165 = f32[256,2,1024]{2,1,0:T(2,128)} reshape(bf16[1,512,1024]{2,1,0:T(8,128)(2,1)} %param.11) | data formatting | bytes 3145728 | tf_op jit(solution)/shard_map/convert_element_type | solution.py:52
  4.2 5.1 %reduce_sum.74 = f32[256,1024]{1,0:T(8,128)} reduce(f32[256,2,1024]{2,1,0:T(2,128)} %reshape.165, f32[]{:T(128)} %constant.55.clone.1), dimensions={1}, to_apply=%region_0.0 | reduce | flops 262144 | bytes 3145732 | tf_op jit(solution)/shard_map/reduce_sum | solution.py:52
  9.3 2.1 multiply_convert_fusion.2
  11.4 2.1 copy.80
  13.5 7.3 %all-to-all-start.1 = ((bf16[256,8,128]{0,2,1:T(8,128)(2,1)}), bf16[256,8,128]{0,2,1:T(8,128)(2,1)}, u32[]{:S(2)}, u32[]{:S(2)}) async-start(bf16[256,8,128]{0,2,1:T(8,128)(2,1)} %bitcast.126), calls=%async_computation.1 | async-start | bytes 1048576 | tf_op jit(solution)/shard_map/all_to_all | solution.py:58
  20.8 1.3 copy.83
  22.1 3.5 %reshape.166 = f32[256,2,1024]{2,1,0:T(2,128)} reshape(bf16[1,512,1024]{2,1,0:T(8,128)(2,1)} %param.10) | data formatting | bytes 3145728 | tf_op jit(solution)/shard_map/convert_element_type | solution.py:49
  25.6 5.1 %reduce_sum.75 = f32[256,1024]{1,0:T(8,128)} reduce(f32[256,2,1024]{2,1,0:T(2,128)} %reshape.166, f32[]{:T(128)} %constant.55.clone.1), dimensions={1}, to_apply=%region_1.0 | reduce | flops 262144 | bytes 3145732 | tf_op jit(solution)/shard_map/reduce_sum | solution.py:49
  30.7 2.1 multiply_convert_fusion.1
  32.8 2.0 copy.82
  34.8 2.4 bitcast_reduce_fusion.1
  37.2 3.2 %copy-done.3 = f32[16,256,512]{2,1,0:T(8,128)} copy-done((f32[16,256,512]{2,1,0:T(8,128)}, f32[16,256,512]{2,1,0:T(8,128)S(1)}, u32[]{:S(2)}) %copy-start.3) | copy-done | bytes 8388632
  40.5 2.0 fusion.16
  42.5 2.4 copy.84
  44.8 6.1 %divide_convert_fusion = bf16[256,16,64]{0,2,1:T(8,128)(2,1)} fusion(bf16[512,16,64]{0,2,1:T(8,128)(2,1)} %bitcast.129, f32[16,256,512]{2,1,0:T(8,128)} %copy-done.3, f32[256,16]{0,1:T(8,128)S(1)} %get-tuple-element.71, f32[256,16]{0,1:T(8,128)S(1)} %fusion.16), kind=kOutput, calls=%fused_computation.30 | convolution fusion | flops 275251200 | bytes 9994240 | tf_op jit(solution)/shard_map/nhm,mhe->nhe/dot_general | solution.py:24
  51.0 6.0 %all-to-all-start.2 = ((bf16[256,8,128]{0,2,1:T(8,128)(2,1)}), bf16[256,8,128]{0,2,1:T(8,128)(2,1)}, u32[]{:S(2)}, u32[]{:S(2)}) async-start(bf16[256,8,128]{0,2,1:T(8,128)(2,1)} %bitcast.131), calls=%async_computation.2 | async-start | bytes 1048576 | tf_op jit(solution)/shard_map/all_to_all | solution.py:59
  57.0 1.3 copy.78
  58.3 12.7 %all-to-all-done.2 = bf16[256,8,128]{0,2,1:T(8,128)(2,1)} async-done(((bf16[256,8,128]{0,2,1:T(8,128)(2,1)}), bf16[256,8,128]{0,2,1:T(8,128)(2,1)}, u32[]{:S(2)}, u32[]{:S(2)}) %all-to-all-start.2) | async-done | bytes 524320 | tf_op jit(solution)/shard_map/all_to_all | solution.py:59
  71.0 4.2 %all-to-all-start = ((bf16[512,8,128]{0,2,1:T(8,128)(2,1)}), bf16[512,8,128]{0,2,1:T(8,128)(2,1)}, u32[]{:S(2)}, u32[]{:S(2)}) async-start(bf16[512,8,128]{0,2,1:T(8,128)(2,1)} %bitcast.124), calls=%async_computation | async-start | bytes 2097152 | tf_op jit(solution)/shard_map/all_to_all | solution.py:57
  75.3 1.3 copy.81
  76.9 1.9 copy.103
  78.8 21.8 %all-to-all-done = bf16[512,8,128]{0,2,1:T(8,128)(2,1)} async-done(((bf16[512,8,128]{0,2,1:T(8,128)(2,1)}), bf16[512,8,128]{0,2,1:T(8,128)(2,1)}, u32[]{:S(2)}, u32[]{:S(2)}) %all-to-all-start) | async-done | bytes 1048608 | tf_op jit(solution)/shard_map/all_to_all | solution.py:57
  100.5 2.3 copy.79
  102.8 89.4 %while.10 = (s32[]{:T(128)}, bf16[4,1024,128]{2,1,0:T(8,128)(2,1)}, bf16[4,1024,128]{2,1,0:T(8,128)(2,1)}, bf16[2048,128]{0,1:T(8,128)(2,1)S(1)}, bf16[2048,128]{0,1:T(8,128)(2,1)}, /*index=5*/s32[]{:T(128)}) while((s32[]{:T(128)}, bf16[4,1024,128]{2,1,0:T(8,128)(2,1)}, bf16[4,1024,128]{2,1,0:T(8,128)(2,1)}, bf16[2048,128]{0,1:T(8,128)(2,1)S(1)}, ...), condition=%wide.region_7.8_spmd, body=%wide.region_4.7_spmd.sunk | while | flops 1107554304 | bytes 121151608 | solution.py:37
  102.8 1.0 constant_dynamic-slice_fusion.2
  104.0 2.5 bitcast_reduce_fusion.3
  106.5 5.7 %copy-done.2 = f32[2,1024,2048]{2,1,0:T(8,128)} copy-done((f32[2,1024,2048]{2,1,0:T(8,128)}, f32[2,1024,2048]{2,1,0:T(8,128)S(1)}, u32[]{:S(2)}) %copy-start.2) | copy-done | bytes 16777240 | tf_op jit(solution)/shard_map/while
  112.2 3.3 %fusion.67 = f32[1024,2]{0,1:T(2,128)S(1)} fusion(f32[2,1024,2048]{2,1,0:T(8,128)S(1)} %get-tuple-element.108, f32[1024,2]{0,1:T(2,128)S(1)} %get-tuple-element.109), kind=kLoop, calls=%fused_computation.6.clone.1 | loop fusion | flops 12580864 | bytes 16793600 | tf_op jit(solution)/shard_map/while/body/eval_jaxpr/reduce_sum | solution.py:23
  115.4 8.9 %fusion.68 = bf16[1024,2,64]{0,2,1:T(8,128)(2,1)S(1)} fusion(bf16[2048,2,64]{0,2,1:T(8,128)(2,1)} %bitcast.110, f32[2,1024,2048]{2,1,0:T(8,128)} %copy-done.2, f32[1024,2]{0,1:T(2,128)S(1)} %get-tuple-element.109, f32[1024,2]{0,1:T(2,128)S(1)} %fusion.67), kind=kOutput, calls=%fused_computation.11.clone.1 | convolution fusion | flops 549715968 | bytes 17580032 | tf_op jit(solution)/shard_map/while/body/eval_jaxpr/nhm,mhe->nhe/dot_general | solution.py:24
  124.5 0.7 constant_dynamic-update-slice_fusion.2
  125.2 1.0 constant_dynamic-slice_fusion.2
  126.3 2.5 bitcast_reduce_fusion.3
  128.8 5.7 %copy-done.2 = f32[2,1024,2048]{2,1,0:T(8,128)} copy-done((f32[2,1024,2048]{2,1,0:T(8,128)}, f32[2,1024,2048]{2,1,0:T(8,128)S(1)}, u32[]{:S(2)}) %copy-start.2) | copy-done | bytes 16777240 | tf_op jit(solution)/shard_map/while
  134.5 3.3 %fusion.67 = f32[1024,2]{0,1:T(2,128)S(1)} fusion(f32[2,1024,2048]{2,1,0:T(8,128)S(1)} %get-tuple-element.108, f32[1024,2]{0,1:T(2,128)S(1)} %get-tuple-element.109), kind=kLoop, calls=%fused_computation.6.clone.1 | loop fusion | flops 12580864 | bytes 16793600 | tf_op jit(solution)/shard_map/while/body/eval_jaxpr/reduce_sum | solution.py:23
  137.8 8.8 %fusion.68 = bf16[1024,2,64]{0,2,1:T(8,128)(2,1)S(1)} fusion(bf16[2048,2,64]{0,2,1:T(8,128)(2,1)} %bitcast.110, f32[2,1024,2048]{2,1,0:T(8,128)} %copy-done.2, f32[1024,2]{0,1:T(2,128)S(1)} %get-tuple-element.109, f32[1024,2]{0,1:T(2,128)S(1)} %fusion.67), kind=kOutput, calls=%fused_computation.11.clone.1 | convolution fusion | flops 549715968 | bytes 17580032 | tf_op jit(solution)/shard_map/while/body/eval_jaxpr/nhm,mhe->nhe/dot_general | solution.py:24
  146.8 0.7 constant_dynamic-update-slice_fusion.2
  147.5 1.0 constant_dynamic-slice_fusion.2
  148.7 2.5 bitcast_reduce_fusion.3
  151.1 5.7 %copy-done.2 = f32[2,1024,2048]{2,1,0:T(8,128)} copy-done((f32[2,1024,2048]{2,1,0:T(8,128)}, f32[2,1024,2048]{2,1,0:T(8,128)S(1)}, u32[]{:S(2)}) %copy-start.2) | copy-done | bytes 16777240 | tf_op jit(solution)/shard_map/while
  156.9 3.3 %fusion.67 = f32[1024,2]{0,1:T(2,128)S(1)} fusion(f32[2,1024,2048]{2,1,0:T(8,128)S(1)} %get-tuple-element.108, f32[1024,2]{0,1:T(2,128)S(1)} %get-tuple-element.109), kind=kLoop, calls=%fused_computation.6.clone.1 | loop fusion | flops 12580864 | bytes 16793600 | tf_op jit(solution)/shard_map/while/body/eval_jaxpr/reduce_sum | solution.py:23
  160.1 8.8 %fusion.68 = bf16[1024,2,64]{0,2,1:T(8,128)(2,1)S(1)} fusion(bf16[2048,2,64]{0,2,1:T(8,128)(2,1)} %bitcast.110, f32[2,1024,2048]{2,1,0:T(8,128)} %copy-done.2, f32[1024,2]{0,1:T(2,128)S(1)} %get-tuple-element.109, f32[1024,2]{0,1:T(2,128)S(1)} %fusion.67), kind=kOutput, calls=%fused_computation.11.clone.1 | convolution fusion | flops 549715968 | bytes 17580032 | tf_op jit(solution)/shard_map/while/body/eval_jaxpr/nhm,mhe->nhe/dot_general | solution.py:24
  169.1 0.7 constant_dynamic-update-slice_fusion.2
  169.9 1.0 constant_dynamic-slice_fusion.2
  171.0 2.5 bitcast_reduce_fusion.3
  173.5 5.7 %copy-done.2 = f32[2,1024,2048]{2,1,0:T(8,128)} copy-done((f32[2,1024,2048]{2,1,0:T(8,128)}, f32[2,1024,2048]{2,1,0:T(8,128)S(1)}, u32[]{:S(2)}) %copy-start.2) | copy-done | bytes 16777240 | tf_op jit(solution)/shard_map/while
  179.2 3.3 %fusion.67 = f32[1024,2]{0,1:T(2,128)S(1)} fusion(f32[2,1024,2048]{2,1,0:T(8,128)S(1)} %get-tuple-element.108, f32[1024,2]{0,1:T(2,128)S(1)} %get-tuple-element.109), kind=kLoop, calls=%fused_computation.6.clone.1 | loop fusion | flops 12580864 | bytes 16793600 | tf_op jit(solution)/shard_map/while/body/eval_jaxpr/reduce_sum | solution.py:23
  182.4 8.8 %fusion.68 = bf16[1024,2,64]{0,2,1:T(8,128)(2,1)S(1)} fusion(bf16[2048,2,64]{0,2,1:T(8,128)(2,1)} %bitcast.110, f32[2,1024,2048]{2,1,0:T(8,128)} %copy-done.2, f32[1024,2]{0,1:T(2,128)S(1)} %get-tuple-element.109, f32[1024,2]{0,1:T(2,128)S(1)} %fusion.67), kind=kOutput, calls=%fused_computation.11.clone.1 | convolution fusion | flops 549715968 | bytes 17580032 | tf_op jit(solution)/shard_map/while/body/eval_jaxpr/nhm,mhe->nhe/dot_general | solution.py:24
  191.5 0.7 constant_dynamic-update-slice_fusion.2
  192.2 3.7 %all-to-all-start.3 = ((bf16[8,512,128]{2,1,0:T(8,128)(2,1)}), bf16[8,512,128]{2,1,0:T(8,128)(2,1)S(1)}, u32[]{:S(2)}, u32[]{:S(2)}) async-start(bf16[8,512,128]{2,1,0:T(8,128)(2,1)} %bitcast.128), calls=%async_computation.3 | async-start | bytes 2097152 | tf_op jit(solution)/shard_map/all_to_all | solution.py:63
  196.6 0.6 gather_fusion
  197.8 0.6 gather_fusion.1
  198.5 0.7 select_convert_fusion
  199.1 22.5 %all-to-all-done.3 = bf16[8,512,128]{2,1,0:T(8,128)(2,1)S(1)} async-done(((bf16[8,512,128]{2,1,0:T(8,128)(2,1)}), bf16[8,512,128]{2,1,0:T(8,128)(2,1)S(1)}, u32[]{:S(2)}, u32[]{:S(2)}) %all-to-all-start.3) | async-done | bytes 1048608 | tf_op jit(solution)/shard_map/all_to_all | solution.py:63
  221.7 3.2 %all-to-all-start.4 = ((bf16[4,2,128]{2,1,0:T(2,128)(2,1)}), bf16[4,2,128]{2,1,0:T(2,128)(2,1)S(1)}, u32[]{:S(2)}, u32[]{:S(2)}) async-start(bf16[4,2,128]{2,1,0:T(2,128)(2,1)} %select_convert_fusion), calls=%async_computation.4 | async-start | bytes 4096 | tf_op jit(solution)/shard_map/all_to_all | solution.py:95
  224.9 1.5 copy.89
  226.4 1.4 multiply_reduce_fusion
  227.8 1.3 copy-done.4
  229.1 0.2 multiply_convert_fusion
  229.4 2.0 gather_fusion.2
  231.4 3.2 %select_select_fusion = bf16[4,2,128,1024]{3,2,1,0:T(8,128)(2,1)} fusion(bf16[4,2,128,1024]{3,2,1,0:T(8,128)(2,1)} %bitcast.118, pred[4,2]{1,0:T(4,128)(4,1)S(1)} %copy.94, pred[4,2]{1,0:T(4,128)(4,1)S(1)} %copy.90), kind=kLoop, calls=%fused_computation.25 | loop fusion | flops 2097152 | bytes 4194320 | tf_op jit(solution)/shard_map/jit(_where)/select_n | solution.py:84
  234.6 4.4 %all-to-all-start.5 = ((bf16[4,2,128,1024]{3,2,1,0:T(8,128)(2,1)}), bf16[4,2,128,1024]{3,2,1,0:T(8,128)(2,1)}, u32[]{:S(2)}, u32[]{:S(2)}) async-start(bf16[4,2,128,1024]{3,2,1,0:T(8,128)(2,1)} %select_select_fusion), calls=%async_computation.5 | async-start | bytes 4194304 | tf_op jit(solution)/shard_map/all_to_all | solution.py:94
  239.3 2.8 %fusion.56 = bf16[1,512,1024]{2,1,0:T(8,128)(2,1)} fusion(f32[1024]{0:T(1024)S(1)} %copy-done.10, f32[512,1024]{1,0:T(8,128)} %copy-done.4, f32[512]{0:T(512)S(1)} %add_rsqrt_fusion), kind=kLoop, calls=%fused_computation.59 | loop fusion | flops 1572864 | bytes 3151872 | tf_op jit(solution)/shard_map/broadcast_in_dim | solution.py:104
  242.1 22.7 %all-to-all-done.5 = bf16[4,2,128,1024]{3,2,1,0:T(8,128)(2,1)} async-done(((bf16[4,2,128,1024]{3,2,1,0:T(8,128)(2,1)}), bf16[4,2,128,1024]{3,2,1,0:T(8,128)(2,1)}, u32[]{:S(2)}, u32[]{:S(2)}) %all-to-all-start.5) | async-done | bytes 2097184 | tf_op jit(solution)/shard_map/all_to_all | solution.py:94
  264.8 2.8 %fusion.36 = bf16[1,128,1024]{2,1,0:T(8,128)(2,1)} fusion(bf16[4,2,128,1024]{3,2,1,0:T(8,128)(2,1)} %all-to-all-done.5, f32[128]{0:T(128)S(1)} %broadcast_maximum_fusion, bf16[4,2,128]{2,0,1:T(4,128)(2,1)S(1)} %copy.95, bf16[128]{0:T(256)(128)(2,1)S(1)} %iota_convert_fusion), kind=kOutput, calls=%fused_computation.35 | convolution fusion | flops 268828672 | bytes 2362112 | tf_op jit(solution)/shard_map/scrf,scfd->rd/dot_general | solution.py:99
  (57 shorter events, 3.1 us)
Async XLA Ops:
  0.6 225.8 %copy-start = (bf16[1024,1024]{1,0:T(8,128)(2,1)S(1)}, bf16[1024,1024]{1,0:T(8,128)(2,1)}, u32[]{:S(2)}) copy-start(bf16[1024,1024]{1,0:T(8,128)(2,1)} %param.13) | copy-start | bytes 6291460
  0.6 20.1 %copy-start.5 = (bf16[1,512,1024]{2,1,0:T(8,128)(2,1)S(1)}, bf16[1,512,1024]{2,1,0:T(8,128)(2,1)}, u32[]{:S(2)}) copy-start(bf16[1,512,1024]{2,1,0:T(8,128)(2,1)} %param.11) | copy-start | bytes 3145732
  13.5 37.5 %all-to-all-start.1 = ((bf16[256,8,128]{0,2,1:T(8,128)(2,1)}), bf16[256,8,128]{0,2,1:T(8,128)(2,1)}, u32[]{:S(2)}, u32[]{:S(2)}) async-start(bf16[256,8,128]{0,2,1:T(8,128)(2,1)} %bitcast.126), calls=%async_computation.1 | async-start | bytes 1048576 | tf_op jit(solution)/shard_map/all_to_all | solution.py:58
  22.1 12.7 %copy-start.7 = (bf16[1,512,1024]{1,2,0:T(8,128)(2,1)S(1)}, bf16[1,512,1024]{1,2,0:T(8,128)(2,1)}, u32[]{:S(2)}) copy-start(bf16[1,512,1024]{1,2,0:T(8,128)(2,1)} %copy.83) | copy-start | bytes 3145732
  37.2 3.2 %copy-start.3 = (f32[16,256,512]{2,1,0:T(8,128)}, f32[16,256,512]{2,1,0:T(8,128)S(1)}, u32[]{:S(2)}) copy-start(f32[16,256,512]{2,1,0:T(8,128)S(1)} %get-tuple-element.72) | copy-start | bytes 25165828
  42.5 14.5 %copy-start.6 = (bf16[1,512,1024]{2,1,0:T(8,128)(2,1)S(1)}, bf16[1,512,1024]{2,1,0:T(8,128)(2,1)}, u32[]{:S(2)}) copy-start(bf16[1,512,1024]{2,1,0:T(8,128)(2,1)} %param.10) | copy-start | bytes 3145732
  51.0 20.1 %all-to-all-start.2 = ((bf16[256,8,128]{0,2,1:T(8,128)(2,1)}), bf16[256,8,128]{0,2,1:T(8,128)(2,1)}, u32[]{:S(2)}, u32[]{:S(2)}) async-start(bf16[256,8,128]{0,2,1:T(8,128)(2,1)} %bitcast.131), calls=%async_computation.2 | async-start | bytes 1048576 | tf_op jit(solution)/shard_map/all_to_all | solution.py:59
  71.0 29.5 %all-to-all-start = ((bf16[512,8,128]{0,2,1:T(8,128)(2,1)}), bf16[512,8,128]{0,2,1:T(8,128)(2,1)}, u32[]{:S(2)}, u32[]{:S(2)}) async-start(bf16[512,8,128]{0,2,1:T(8,128)(2,1)} %bitcast.124), calls=%async_computation | async-start | bytes 2097152 | tf_op jit(solution)/shard_map/all_to_all | solution.py:57
  102.8 93.1 %copy-start.11 = (s32[1,4,1]{1,2,0:T(1,128)S(1)}, s32[1,4,1]{1,2,0:T(1,128)}, u32[]{:S(2)}) copy-start(s32[1,4,1]{1,2,0:T(1,128)} %param.15) | copy-start | bytes 52
  102.8 93.8 %copy-start.1 = (s32[1,4]{1,0:T(1,128)S(1)}, s32[1,4]{1,0:T(1,128)}, u32[]{:S(2)}) copy-start(s32[1,4]{1,0:T(1,128)} %param.16) | copy-start | bytes 52
  102.8 95.0 %copy-start.9 = (s32[1,4,128]{2,1,0:T(4,128)S(1)}, s32[1,4,128]{2,1,0:T(4,128)}, u32[]{:S(2)}) copy-start(s32[1,4,128]{2,1,0:T(4,128)} %param.17) | copy-start | bytes 6148
  106.5 5.7 %copy-start.2 = (f32[2,1024,2048]{2,1,0:T(8,128)}, f32[2,1024,2048]{2,1,0:T(8,128)S(1)}, u32[]{:S(2)}) copy-start(f32[2,1024,2048]{2,1,0:T(8,128)S(1)} %get-tuple-element.108) | copy-start | bytes 50331652 | tf_op jit(solution)/shard_map/while
  128.8 5.7 %copy-start.2 = (f32[2,1024,2048]{2,1,0:T(8,128)}, f32[2,1024,2048]{2,1,0:T(8,128)S(1)}, u32[]{:S(2)}) copy-start(f32[2,1024,2048]{2,1,0:T(8,128)S(1)} %get-tuple-element.108) | copy-start | bytes 50331652 | tf_op jit(solution)/shard_map/while
  151.1 5.7 %copy-start.2 = (f32[2,1024,2048]{2,1,0:T(8,128)}, f32[2,1024,2048]{2,1,0:T(8,128)S(1)}, u32[]{:S(2)}) copy-start(f32[2,1024,2048]{2,1,0:T(8,128)S(1)} %get-tuple-element.108) | copy-start | bytes 50331652 | tf_op jit(solution)/shard_map/while
  173.5 5.7 %copy-start.2 = (f32[2,1024,2048]{2,1,0:T(8,128)}, f32[2,1024,2048]{2,1,0:T(8,128)S(1)}, u32[]{:S(2)}) copy-start(f32[2,1024,2048]{2,1,0:T(8,128)S(1)} %get-tuple-element.108) | copy-start | bytes 50331652 | tf_op jit(solution)/shard_map/while
  192.2 36.9 %copy-start.10 = (f32[1024]{0:T(1024)S(1)}, f32[1024]{0:T(1024)}, u32[]{:S(2)}) copy-start(f32[1024]{0:T(1024)} %param.14) | copy-start | bytes 12292
  192.2 29.5 %all-to-all-start.3 = ((bf16[8,512,128]{2,1,0:T(8,128)(2,1)}), bf16[8,512,128]{2,1,0:T(8,128)(2,1)S(1)}, u32[]{:S(2)}, u32[]{:S(2)}) async-start(bf16[8,512,128]{2,1,0:T(8,128)(2,1)} %bitcast.128), calls=%async_computation.3 | async-start | bytes 2097152 | tf_op jit(solution)/shard_map/all_to_all | solution.py:63
  221.7 3.2 %copy-start.8 = (bf16[8,512,128]{2,1,0:T(8,128)(2,1)}, bf16[8,512,128]{2,1,0:T(8,128)(2,1)S(1)}, u32[]{:S(2)}) copy-start(bf16[8,512,128]{2,1,0:T(8,128)(2,1)S(1)} %all-to-all-done.3) | copy-start | bytes 3145732
  221.7 12.9 %all-to-all-start.4 = ((bf16[4,2,128]{2,1,0:T(2,128)(2,1)}), bf16[4,2,128]{2,1,0:T(2,128)(2,1)S(1)}, u32[]{:S(2)}, u32[]{:S(2)}) async-start(bf16[4,2,128]{2,1,0:T(2,128)(2,1)} %select_convert_fusion), calls=%async_computation.4 | async-start | bytes 4096 | tf_op jit(solution)/shard_map/all_to_all | solution.py:95
  227.8 1.4 copy-start.4
  234.6 30.2 %all-to-all-start.5 = ((bf16[4,2,128,1024]{3,2,1,0:T(8,128)(2,1)}), bf16[4,2,128,1024]{3,2,1,0:T(8,128)(2,1)}, u32[]{:S(2)}, u32[]{:S(2)}) async-start(bf16[4,2,128,1024]{3,2,1,0:T(8,128)(2,1)} %select_select_fusion), calls=%async_computation.5 | async-start | bytes 4194304 | tf_op jit(solution)/shard_map/all_to_all | solution.py:94
where the time goes:
time: 269 us; the launch traced here: 268 us
  waiting for transfers between devices  79.7 us (30%)
  local copies, waits for them, and re-layouts  62.9 us (23%)
  matrix products  58 us (22%)
  other arithmetic  37.1 us (14%)
  starting transfers between devices  28.9 us (11%)
    dot_general x5, matrix products, mix_heads(): jnp.einsum('nhm,mhe->nhe', weights.astype(jnp.bfloat16), value_heads, pre...  41.5 us
    while x8, local copies, waits for them, and re-layouts  22.9 us
    all_to_all x1, waiting for transfers between devices, local(): lax.all_to_all(sent_rows, 'pack', split_axis=0, concat_axis=0, tiled=True)  22.7 us
    all_to_all x1, waiting for transfers between devices, local(): lax.all_to_all(head_result, 'tm', split_axis=0, concat_axis=1, tiled=True)  22.5 us
    all_to_all x1, waiting for transfers between devices, local(): lax.all_to_all(frame_q, 'tm', split_axis=1, concat_axis=0, tiled=True)  21.8 us
    reduce_sum x5, other arithmetic, mix_heads(): totals = jnp.sum(weights, axis=-1)  15 us
    all_to_all x1, waiting for transfers between devices, local(): lax.all_to_all(mark_values, 'tm', split_axis=1, concat_axis=0, tiled=True)  12.7 us
    dot_general x5, matrix products, mix_heads(): jnp.einsum('nhe,mhe->nhm', query_heads, key_heads, preferred_element_type...  12.3 us
  transfers between devices with their start and end apart: 6, of which 4 were waited for; matrix products, arithmetic and copies ran while one was open for 17% of the time, Pallas kernels for 0%

commit v1 on v0

--- a/solution.py
+++ b/solution.py
@@ -3,11 +3,26 @@
 import jax.numpy as jnp
 from jax import lax
 from jax.sharding import PartitionSpec as P
+from jax.lax import axis_index, axis_size, ppermute
 
 HEADS = 16
 LANDMARKS = 256
 BLOCK = 128
 POOL_DEV = 128
+
+
+def groups_draft(payload, along_dim, xin):
+    met_up = payload.shape
+    opened = payload.reshape(
+        *met_up[:along_dim], xin, met_up[along_dim] // xin, *met_up[along_dim + 1 :]
+    )
+    return jnp.moveaxis(opened, along_dim, 0)
+
+
+def press_samples_now(sample, where_dim):
+    value_now = list(sample.shape[1:])
+    value_now[where_dim] *= sample.shape[0]
+    return jnp.moveaxis(sample, 0, where_dim).reshape(value_now)
 
 
 def mix_heads(query_rows, mark_keys, mark_values, head_count):
@@ -53,10 +68,25 @@
         frame_k.reshape(LANDMARKS, span, model_width), axis=1, dtype=jnp.float32
     ).astype(jnp.bfloat16)
     mark_values = mix_heads(mark_queries, frame_k, frame_v, HEADS)
+
+    def drive_things_in(view, arr_in, row_axis, in_array):
+        arr_now, piece_out = (axis_size(row_axis), axis_index(row_axis))
+        tall = groups_draft(arr_in, in_array, arr_now)
+        samples = [tall[piece_out]]
+        for jj in range(1, arr_now):
+            x_now = tall[(piece_out + jj) % arr_now]
+            samples.append(
+                ppermute(
+                    x_now, row_axis, [(src_i, (src_i + jj) % arr_now) for src_i in range(arr_now)]
+                )
+            )
+        tall = jnp.stack(samples, 0)[(piece_out - jnp.arange(arr_now)) % arr_now]
+        return press_samples_now(tall, view)
+
     spread_q, spread_k, spread_v = (
         lax.all_to_all(frame_q, "tm", split_axis=1, concat_axis=0, tiled=True),
         lax.all_to_all(mark_keys, "tm", split_axis=1, concat_axis=0, tiled=True),
-        lax.all_to_all(mark_values, "tm", split_axis=1, concat_axis=0, tiled=True),
+        drive_things_in(0, mark_values, "tm", 1),
     )
     local_heads = HEADS // lax.axis_size("tm")
     head_result = mix_blocked(spread_q, spread_k, spread_v, local_heads)

time: 269 us -> 254 us (0.944)
  waiting for transfers between devices: 79.7 us -> 56 us
  starting transfers between devices: 28.9 us -> 42.1 us
  local copies, waits for them, and re-layouts: 62.9 us -> 58.5 us
    all_to_all x1, waiting for transfers between devices: 21.8 us -> 3.57 us  [local(): lax.all_to_all(frame_q, 'tm', split_axis=1, concat_axis=0, tiled=True)]
    ppermute x0 -> x7, starting transfers between devices: none -> 15.1 us  [drive_things_in(): ppermute(x_now, row_axis, [(src_i, (src_i + jj) % arr_now) for src_i in r...]
    while x8, local copies, waits for them, and re-layouts: 22.9 us -> 9.79 us
    all_to_all x1 -> x0, waiting for transfers between devices: 12.7 us -> none  [local(): lax.all_to_all(mark_values, 'tm', split_axis=1, concat_axis=0, tiled=True)]
    ppermute x0 -> x7, waiting for transfers between devices: none -> 9.34 us  [drive_things_in(): ppermute(x_now, row_axis, [(src_i, (src_i + jj) % arr_now) for src_i in r...]
    another operation x0 -> x11, local copies, waits for them, and re-layouts: none -> 6.2 us
    all_to_all x1 -> x0, starting transfers between devices: 5.99 us -> none  [local(): lax.all_to_all(mark_values, 'tm', split_axis=1, concat_axis=0, tiled=True)]
    all_to_all x1, starting transfers between devices: 3.69 us -> 7.89 us  [local(): lax.all_to_all(head_result, 'tm', split_axis=0, concat_axis=1, tiled=True)]
  transfers between devices with their start and end apart: 6 -> 12, of which waited for: 4 -> 5; matrix products, arithmetic and copies ran while one was open for 17% -> 21% of each run, Pallas kernels for 0% -> 0%
where the time goes in v1:
time: 254 us; the launch traced here: 252 us
  local copies, waits for them, and re-layouts  58.5 us (23%)
  matrix products  57.2 us (23%)
  waiting for transfers between devices  56 us (22%)
  starting transfers between devices  42.1 us (17%)
  other arithmetic  37.1 us (15%)
    dot_general x5, matrix products, mix_heads(): jnp.einsum('nhm,mhe->nhe', weights.astype(jnp.bfloat16), value_heads, pre...  40.7 us
    all_to_all x1, waiting for transfers between devices, local(): lax.all_to_all(sent_rows, 'pack', split_axis=0, concat_axis=0, tiled=True)  22.7 us
    all_to_all x1, waiting for transfers between devices, local(): lax.all_to_all(head_result, 'tm', split_axis=0, concat_axis=1, tiled=True)  20.4 us
    reduce_sum x5, other arithmetic, mix_heads(): totals = jnp.sum(weights, axis=-1)  15.1 us
    ppermute x7, starting transfers between devices, drive_things_in(): ppermute(x_now, row_axis, [(src_i, (src_i + jj) % arr_now) for src_i in r...  15.1 us
    unnamed x34, local copies, waits for them, and re-layouts  13.1 us
    dot_general x5, matrix products, mix_heads(): jnp.einsum('nhe,mhe->nhm', query_heads, key_heads, preferred_element_type...  12.3 us
    while x8, local copies, waits for them, and re-layouts  9.79 us
  transfers between devices with their start and end apart: 12, of which 5 were waited for; matrix products, arithmetic and copies ran while one was open for 21% of the time, Pallas kernels for 0%

profile of v1, /device:TPU:0, one launch (start us, length us, event | category | flops | bytes accessed | tf_op | source)
XLA Modules:
  0.0 252.2 jit_solution(11233399093312790226)
XLA Ops:
  0.7 3.6 %reshape.224 = f32[256,2,1024]{2,1,0:T(2,128)} reshape(bf16[1,512,1024]{2,1,0:T(8,128)(2,1)} %param.11) | data formatting | bytes 3145728 | tf_op jit(solution)/shard_map/convert_element_type | solution.py:67
  4.2 5.1 %reduce_sum.74 = f32[256,1024]{1,0:T(8,128)} reduce(f32[256,2,1024]{2,1,0:T(2,128)} %reshape.224, f32[]{:T(128)} %constant.128.clone.1), dimensions={1}, to_apply=%region_0.0 | reduce | flops 262144 | bytes 3145732 | tf_op jit(solution)/shard_map/reduce_sum | solution.py:67
  9.3 2.1 multiply_convert_fusion.2
  11.4 2.1 copy.111
  13.4 7.3 %all-to-all-start.1 = ((bf16[256,8,128]{0,2,1:T(8,128)(2,1)}), bf16[256,8,128]{0,2,1:T(8,128)(2,1)}, u32[]{:S(2)}, u32[]{:S(2)}) async-start(bf16[256,8,128]{0,2,1:T(8,128)(2,1)} %bitcast.157), calls=%async_computation.1 | async-start | bytes 1048576 | tf_op jit(solution)/shard_map/all_to_all | solution.py:88
  20.7 1.3 copy.114
  22.1 3.5 %reshape.225 = f32[256,2,1024]{2,1,0:T(2,128)} reshape(bf16[1,512,1024]{2,1,0:T(8,128)(2,1)} %param.10) | data formatting | bytes 3145728 | tf_op jit(solution)/shard_map/convert_element_type | solution.py:64
  25.5 5.1 %reduce_sum.75 = f32[256,1024]{1,0:T(8,128)} reduce(f32[256,2,1024]{2,1,0:T(2,128)} %reshape.225, f32[]{:T(128)} %constant.128.clone.1), dimensions={1}, to_apply=%region_1.0 | reduce | flops 262144 | bytes 3145732 | tf_op jit(solution)/shard_map/reduce_sum | solution.py:64
  30.6 2.1 multiply_convert_fusion.1
  32.7 2.0 copy.113
  34.7 2.4 bitcast_reduce_fusion.1
  37.2 3.2 %copy-done.3 = f32[16,256,512]{2,1,0:T(8,128)} copy-done((f32[16,256,512]{2,1,0:T(8,128)}, f32[16,256,512]{2,1,0:T(8,128)S(1)}, u32[]{:S(2)}) %copy-start.3) | copy-done | bytes 8388632
  40.4 2.0 fusion.16
  42.5 2.4 copy.115
  44.9 5.3 %divide_convert_fusion = bf16[256,16,64]{0,2,1:T(8,128)(2,1)S(1)} fusion(bf16[512,16,64]{0,2,1:T(8,128)(2,1)} %bitcast.160, f32[16,256,512]{2,1,0:T(8,128)} %copy-done.3, f32[256,16]{0,1:T(8,128)S(1)} %get-tuple-element.79, f32[256,16]{0,1:T(8,128)S(1)} %fusion.16), kind=kOutput, calls=%fused_computation.31 | convolution fusion | flops 275251200 | bytes 9994240 | tf_op jit(solution)/shard_map/nhm,mhe->nhe/dot_general | solution.py:39
  50.9 1.6 copy.117
  52.5 2.0 collective-permute-start
  54.5 1.6 copy.118
  56.1 1.5 collective-permute-start.1
  58.3 2.4 collective-permute-start.2
  60.7 1.5 collective-permute-start.3
  62.4 2.4 collective-permute-start.4
  64.8 1.3 copy.109
  66.2 4.2 %all-to-all-start = ((bf16[512,8,128]{0,2,1:T(8,128)(2,1)}), bf16[512,8,128]{0,2,1:T(8,128)(2,1)}, u32[]{:S(2)}, u32[]{:S(2)}) async-start(bf16[512,8,128]{0,2,1:T(8,128)(2,1)} %bitcast.154), calls=%async_computation | async-start | bytes 2097152 | tf_op jit(solution)/shard_map/all_to_all | solution.py:87
  70.8 3.8 %collective-permute-start.5 = (bf16[256,128]{1,0:T(8,128)(2,1)S(1)}, bf16[256,128]{1,0:T(8,128)(2,1)S(1)}, u32[]{:S(2)}, u32[]{:S(2)}) collective-permute-start(bf16[256,128]{1,0:T(8,128)(2,1)S(1)} %bitcast.169), channel_id=1, source_target_pairs={{0,24},{4,28},{8,0},{12,4},{16,8},{20,12},{24,16},{28,20},{1,25},{... | collective-permute-start | bytes 196616 | tf_op jit(solution)/shard_map/ppermute | solution.py:79
  75.4 1.5 collective-permute-start.6
  79.5 8.6 %collective-permute-done.5 = bf16[256,128]{1,0:T(8,128)(2,1)S(1)} collective-permute-done((bf16[256,128]{1,0:T(8,128)(2,1)S(1)}, bf16[256,128]{1,0:T(8,128)(2,1)S(1)}, u32[]{:S(2)}, u32[]{:S(2)}) %collective-permute-start.5) | collective-permute-done | bytes 65568 | tf_op jit(solution)/shard_map/ppermute | solution.py:79
  90.0 1.1 reshape_reshape.3
  91.0 1.3 copy.112
  92.6 3.6 %all-to-all-done = bf16[512,8,128]{0,2,1:T(8,128)(2,1)} async-done(((bf16[512,8,128]{0,2,1:T(8,128)(2,1)}), bf16[512,8,128]{0,2,1:T(8,128)(2,1)}, u32[]{:S(2)}, u32[]{:S(2)}) %all-to-all-start) | async-done | bytes 1048608 | tf_op jit(solution)/shard_map/all_to_all | solution.py:87
  96.2 2.3 copy.110
  98.4 76.4 %while.11 = (s32[]{:T(128)}, bf16[4,1024,128]{2,1,0:T(8,128)(2,1)}, bf16[4,1024,128]{2,1,0:T(8,128)(2,1)}, bf16[2048,128]{0,1:T(8,128)(2,1)S(1)}, bf16[8,256,128...) while((s32[]{:T(128)}, bf16[4,1024,128]{2,1,0:T(8,128)(2,1)}, ...), condition=%wide.wide.region_7.8_spmd, body=%wide.wide.region_4.7_spmd.sunk | while | flops 1107554304 | bytes 121152104 | solution.py:52
  98.4 1.0 constant_dynamic-slice_fusion.11
  99.6 2.5 bitcast_reduce_fusion.4
  102.1 3.3 %fusion.75 = f32[1024,2]{0,1:T(2,128)S(1)} fusion(f32[2,1024,2048]{2,1,0:T(8,128)S(1)} %get-tuple-element.144, f32[1024,2]{0,1:T(2,128)S(1)} %get-tuple-element.145), kind=kLoop, calls=%fused_computation.7.clone.clone.1 | loop fusion | flops 12580864 | bytes 16793600 | tf_op jit(solution)/shard_map/while/body/eval_jaxpr/reduce_sum | solution.py:38
  105.3 2.4 copy-done.2
  107.8 8.8 %fusion.76 = bf16[1024,2,64]{0,2,1:T(8,128)(2,1)S(1)} fusion(bf16[2048,2,64]{0,2,1:T(8,128)(2,1)} %get-tuple-element.165, f32[2,1024,2048]{2,1,0:T(8,128)} %copy-done.2, f32[1024,2]{0,1:T(2,128)S(1)} %get-tuple-element.145, f32[1024,2]{0,1:T(2,128)S(1)} %fusion.75), kind=kOutput, calls=%fused_computation.12.clone.clone.1 | convolution fusion | flops 549715968 | bytes 17580032 | tf_op jit(solution)/shard_map/while/body/eval_jaxpr/nhm,mhe->nhe/dot_general | solution.py:39
  117.6 1.0 constant_dynamic-slice_fusion.11
  118.7 2.5 bitcast_reduce_fusion.4
  121.2 3.3 %fusion.75 = f32[1024,2]{0,1:T(2,128)S(1)} fusion(f32[2,1024,2048]{2,1,0:T(8,128)S(1)} %get-tuple-element.144, f32[1024,2]{0,1:T(2,128)S(1)} %get-tuple-element.145), kind=kLoop, calls=%fused_computation.7.clone.clone.1 | loop fusion | flops 12580864 | bytes 16793600 | tf_op jit(solution)/shard_map/while/body/eval_jaxpr/reduce_sum | solution.py:38
  124.4 2.4 copy-done.2
  126.9 8.8 %fusion.76 = bf16[1024,2,64]{0,2,1:T(8,128)(2,1)S(1)} fusion(bf16[2048,2,64]{0,2,1:T(8,128)(2,1)} %get-tuple-element.165, f32[2,1024,2048]{2,1,0:T(8,128)} %copy-done.2, f32[1024,2]{0,1:T(2,128)S(1)} %get-tuple-element.145, f32[1024,2]{0,1:T(2,128)S(1)} %fusion.75), kind=kOutput, calls=%fused_computation.12.clone.clone.1 | convolution fusion | flops 549715968 | bytes 17580032 | tf_op jit(solution)/shard_map/while/body/eval_jaxpr/nhm,mhe->nhe/dot_general | solution.py:39
  136.6 1.0 constant_dynamic-slice_fusion.11
  137.8 2.5 bitcast_reduce_fusion.4
  140.2 3.3 %fusion.75 = f32[1024,2]{0,1:T(2,128)S(1)} fusion(f32[2,1024,2048]{2,1,0:T(8,128)S(1)} %get-tuple-element.144, f32[1024,2]{0,1:T(2,128)S(1)} %get-tuple-element.145), kind=kLoop, calls=%fused_computation.7.clone.clone.1 | loop fusion | flops 12580864 | bytes 16793600 | tf_op jit(solution)/shard_map/while/body/eval_jaxpr/reduce_sum | solution.py:38
  143.5 2.4 copy-done.2
  146.0 8.8 %fusion.76 = bf16[1024,2,64]{0,2,1:T(8,128)(2,1)S(1)} fusion(bf16[2048,2,64]{0,2,1:T(8,128)(2,1)} %get-tuple-element.165, f32[2,1024,2048]{2,1,0:T(8,128)} %copy-done.2, f32[1024,2]{0,1:T(2,128)S(1)} %get-tuple-element.145, f32[1024,2]{0,1:T(2,128)S(1)} %fusion.75), kind=kOutput, calls=%fused_computation.12.clone.clone.1 | convolution fusion | flops 549715968 | bytes 17580032 | tf_op jit(solution)/shard_map/while/body/eval_jaxpr/nhm,mhe->nhe/dot_general | solution.py:39
  155.7 1.0 constant_dynamic-slice_fusion.11
  156.8 2.5 bitcast_reduce_fusion.4
  159.3 3.3 %fusion.75 = f32[1024,2]{0,1:T(2,128)S(1)} fusion(f32[2,1024,2048]{2,1,0:T(8,128)S(1)} %get-tuple-element.144, f32[1024,2]{0,1:T(2,128)S(1)} %get-tuple-element.145), kind=kLoop, calls=%fused_computation.7.clone.clone.1 | loop fusion | flops 12580864 | bytes 16793600 | tf_op jit(solution)/shard_map/while/body/eval_jaxpr/reduce_sum | solution.py:38
  162.6 2.4 copy-done.2
  165.0 8.8 %fusion.76 = bf16[1024,2,64]{0,2,1:T(8,128)(2,1)S(1)} fusion(bf16[2048,2,64]{0,2,1:T(8,128)(2,1)} %get-tuple-element.165, f32[2,1024,2048]{2,1,0:T(8,128)} %copy-done.2, f32[1024,2]{0,1:T(2,128)S(1)} %get-tuple-element.145, f32[1024,2]{0,1:T(2,128)S(1)} %fusion.75), kind=kOutput, calls=%fused_computation.12.clone.clone.1 | convolution fusion | flops 549715968 | bytes 17580032 | tf_op jit(solution)/shard_map/while/body/eval_jaxpr/nhm,mhe->nhe/dot_general | solution.py:39
  174.8 7.9 %all-to-all-start.2 = ((bf16[8,512,128]{2,1,0:T(8,128)(2,1)}), bf16[8,512,128]{2,1,0:T(8,128)(2,1)S(1)}, u32[]{:S(2)}, u32[]{:S(2)}) async-start(bf16[8,512,128]{2,1,0:T(8,128)(2,1)} %bitcast.159), calls=%async_computation.2 | async-start | bytes 2097152 | tf_op jit(solution)/shard_map/all_to_all | solution.py:93
  185.9 20.4 %all-to-all-done.2 = bf16[8,512,128]{2,1,0:T(8,128)(2,1)S(1)} async-done(((bf16[8,512,128]{2,1,0:T(8,128)(2,1)}), bf16[8,512,128]{2,1,0:T(8,128)(2,1)S(1)}, u32[]{:S(2)}, u32[]{:S(2)}) %all-to-all-start.2) | async-done | bytes 1048608 | tf_op jit(solution)/shard_map/all_to_all | solution.py:93
  206.3 3.2 %all-to-all-start.3 = ((bf16[4,2,128]{2,1,0:T(2,128)(2,1)}), bf16[4,2,128]{2,1,0:T(2,128)(2,1)S(1)}, u32[]{:S(2)}, u32[]{:S(2)}) async-start(bf16[4,2,128]{2,1,0:T(2,128)(2,1)} %select_convert_fusion), calls=%async_computation.3 | async-start | bytes 4096 | tf_op jit(solution)/shard_map/all_to_all | solution.py:125
  209.6 1.5 copy.128
  211.1 1.4 multiply_reduce_fusion
  212.5 1.3 copy-done.4
  214.0 2.0 gather_fusion.3
  216.0 3.2 %select_select_fusion = bf16[4,2,128,1024]{3,2,1,0:T(8,128)(2,1)} fusion(bf16[4,2,128,1024]{3,2,1,0:T(8,128)(2,1)} %bitcast.149, pred[4,2]{1,0:T(4,128)(4,1)S(1)} %copy.133, pred[4,2]{1,0:T(4,128)(4,1)S(1)} %copy.129), kind=kLoop, calls=%fused_computation.26 | loop fusion | flops 2097152 | bytes 4194320 | tf_op jit(solution)/shard_map/jit(_where)/select_n | solution.py:114
  219.2 4.4 %all-to-all-start.4 = ((bf16[4,2,128,1024]{3,2,1,0:T(8,128)(2,1)}), bf16[4,2,128,1024]{3,2,1,0:T(8,128)(2,1)}, u32[]{:S(2)}, u32[]{:S(2)}) async-start(bf16[4,2,128,1024]{3,2,1,0:T(8,128)(2,1)} %select_select_fusion), calls=%async_computation.4 | async-start | bytes 4194304 | tf_op jit(solution)/shard_map/all_to_all | solution.py:124
  223.9 2.8 %fusion.58 = bf16[1,512,1024]{2,1,0:T(8,128)(2,1)} fusion(f32[1024]{0:T(1024)S(1)} %copy-done.11, f32[512,1024]{1,0:T(8,128)} %copy-done.4, f32[512]{0:T(512)S(1)} %add_rsqrt_fusion), kind=kLoop, calls=%fused_computation.83 | loop fusion | flops 1572864 | bytes 3151872 | tf_op jit(solution)/shard_map/broadcast_in_dim | solution.py:134
  226.7 22.7 %all-to-all-done.4 = bf16[4,2,128,1024]{3,2,1,0:T(8,128)(2,1)} async-done(((bf16[4,2,128,1024]{3,2,1,0:T(8,128)(2,1)}), bf16[4,2,128,1024]{3,2,1,0:T(8,128)(2,1)}, u32[]{:S(2)}, u32[]{:S(2)}) %all-to-all-start.4) | async-done | bytes 2097184 | tf_op jit(solution)/shard_map/all_to_all | solution.py:124
  249.4 2.8 %fusion.36 = bf16[1,128,1024]{2,1,0:T(8,128)(2,1)} fusion(bf16[4,2,128,1024]{3,2,1,0:T(8,128)(2,1)} %all-to-all-done.4, f32[128]{0:T(128)S(1)} %broadcast_maximum_fusion, bf16[4,2,128]{2,0,1:T(4,128)(2,1)S(1)} %copy.134, bf16[128]{0:T(256)(128)(2,1)S(1)} %iota_convert_fusion), kind=kOutput, calls=%fused_computation.36 | convolution fusion | flops 268828672 | bytes 2362112 | tf_op jit(solution)/shard_map/scrf,scfd->rd/dot_general | solution.py:129
  (92 shorter events, 15.3 us)
Async XLA Ops:
  0.6 210.4 %copy-start = (bf16[1024,1024]{1,0:T(8,128)(2,1)S(1)}, bf16[1024,1024]{1,0:T(8,128)(2,1)}, u32[]{:S(2)}) copy-start(bf16[1024,1024]{1,0:T(8,128)(2,1)} %param.13) | copy-start | bytes 6291460
  0.6 20.1 %copy-start.5 = (bf16[1,512,1024]{2,1,0:T(8,128)(2,1)S(1)}, bf16[1,512,1024]{2,1,0:T(8,128)(2,1)}, u32[]{:S(2)}) copy-start(bf16[1,512,1024]{2,1,0:T(8,128)(2,1)} %param.11) | copy-start | bytes 3145732
  13.4 52.8 %all-to-all-start.1 = ((bf16[256,8,128]{0,2,1:T(8,128)(2,1)}), bf16[256,8,128]{0,2,1:T(8,128)(2,1)}, u32[]{:S(2)}, u32[]{:S(2)}) async-start(bf16[256,8,128]{0,2,1:T(8,128)(2,1)} %bitcast.157), calls=%async_computation.1 | async-start | bytes 1048576 | tf_op jit(solution)/shard_map/all_to_all | solution.py:88
  22.1 12.7 %copy-start.7 = (bf16[1,512,1024]{1,2,0:T(8,128)(2,1)S(1)}, bf16[1,512,1024]{1,2,0:T(8,128)(2,1)}, u32[]{:S(2)}) copy-start(bf16[1,512,1024]{1,2,0:T(8,128)(2,1)} %copy.114) | copy-start | bytes 3145732
  37.2 3.2 %copy-start.3 = (f32[16,256,512]{2,1,0:T(8,128)}, f32[16,256,512]{2,1,0:T(8,128)S(1)}, u32[]{:S(2)}) copy-start(f32[16,256,512]{2,1,0:T(8,128)S(1)} %get-tuple-element.80) | copy-start | bytes 25165828
  42.5 22.3 %copy-start.6 = (bf16[1,512,1024]{2,1,0:T(8,128)(2,1)S(1)}, bf16[1,512,1024]{2,1,0:T(8,128)(2,1)}, u32[]{:S(2)}) copy-start(bf16[1,512,1024]{2,1,0:T(8,128)(2,1)} %param.10) | copy-start | bytes 3145732
  52.5 18.3 %collective-permute-start = (bf16[256,128]{1,0:T(8,128)(2,1)}, bf16[256,128]{1,0:T(8,128)(2,1)}, u32[]{:S(2)}, u32[]{:S(2)}) collective-permute-start(bf16[256,128]{1,0:T(8,128)(2,1)} %bitcast.167), channel_id=1, source_target_pairs={{0,4},{4,8},{8,12},{12,16},{16,20},{20,24},{24,28},{28,0},{1,5},{5... | collective-permute-start | bytes 196616 | tf_op jit(solution)/shard_map/ppermute | solution.py:79
  56.1 19.4 %collective-permute-start.1 = (bf16[256,128]{1,0:T(8,128)(2,1)}, bf16[256,128]{1,0:T(8,128)(2,1)}, u32[]{:S(2)}, u32[]{:S(2)}) collective-permute-start(bf16[256,128]{1,0:T(8,128)(2,1)} %bitcast.166), channel_id=1, source_target_pairs={{0,8},{4,12},{8,16},{12,20},{16,24},{20,28},{24,0},{28,4},{1,9},{5... | collective-permute-start | bytes 196616 | tf_op jit(solution)/shard_map/ppermute | solution.py:79
  58.3 19.5 %collective-permute-start.2 = (bf16[256,128]{1,0:T(8,128)(2,1)}, bf16[256,128]{1,0:T(8,128)(2,1)}, u32[]{:S(2)}, u32[]{:S(2)}) collective-permute-start(bf16[256,128]{1,0:T(8,128)(2,1)} %bitcast.165), channel_id=1, source_target_pairs={{0,12},{4,16},{8,20},{12,24},{16,28},{20,0},{24,4},{28,8},{1,13},{... | collective-permute-start | bytes 196616 | tf_op jit(solution)/shard_map/ppermute | solution.py:79
  60.7 17.9 %collective-permute-start.3 = (bf16[256,128]{1,0:T(8,128)(2,1)S(1)}, bf16[256,128]{1,0:T(8,128)(2,1)}, u32[]{:S(2)}, u32[]{:S(2)}) collective-permute-start(bf16[256,128]{1,0:T(8,128)(2,1)S(1)} %bitcast.164), channel_id=1, source_target_pairs={{0,16},{4,20},{8,24},{12,28},{16,0},{20,4},{24,8},{28,12},{1,17},{... | collective-permute-start | bytes 196616 | tf_op jit(solution)/shard_map/ppermute | solution.py:79
  62.4 17.1 %collective-permute-start.4 = (bf16[256,128]{1,0:T(8,128)(2,1)S(1)}, bf16[256,128]{1,0:T(8,128)(2,1)S(1)}, u32[]{:S(2)}, u32[]{:S(2)}) collective-permute-start(bf16[256,128]{1,0:T(8,128)(2,1)S(1)} %bitcast.163), channel_id=1, source_target_pairs={{0,20},{4,24},{8,28},{12,0},{16,4},{20,8},{24,12},{28,16},{1,21},{... | collective-permute-start | bytes 196616 | tf_op jit(solution)/shard_map/ppermute | solution.py:79
  66.2 29.9 %all-to-all-start = ((bf16[512,8,128]{0,2,1:T(8,128)(2,1)}), bf16[512,8,128]{0,2,1:T(8,128)(2,1)}, u32[]{:S(2)}, u32[]{:S(2)}) async-start(bf16[512,8,128]{0,2,1:T(8,128)(2,1)} %bitcast.154), calls=%async_computation | async-start | bytes 2097152 | tf_op jit(solution)/shard_map/all_to_all | solution.py:87
  70.8 17.4 %collective-permute-start.5 = (bf16[256,128]{1,0:T(8,128)(2,1)S(1)}, bf16[256,128]{1,0:T(8,128)(2,1)S(1)}, u32[]{:S(2)}, u32[]{:S(2)}) collective-permute-start(bf16[256,128]{1,0:T(8,128)(2,1)S(1)} %bitcast.169), channel_id=1, source_target_pairs={{0,24},{4,28},{8,0},{12,4},{16,8},{20,12},{24,16},{28,20},{1,25},{... | collective-permute-start | bytes 196616 | tf_op jit(solution)/shard_map/ppermute | solution.py:79
  75.4 13.5 %collective-permute-start.6 = (bf16[256,128]{1,0:T(8,128)(2,1)S(1)}, bf16[256,128]{1,0:T(8,128)(2,1)S(1)}, u32[]{:S(2)}, u32[]{:S(2)}) collective-permute-start(bf16[256,128]{1,0:T(8,128)(2,1)S(1)} %bitcast.168), channel_id=1, source_target_pairs={{0,28},{4,0},{8,4},{12,8},{16,12},{20,16},{24,20},{28,24},{1,29},{... | collective-permute-start | bytes 196616 | tf_op jit(solution)/shard_map/ppermute | solution.py:79
  90.0 2.4 copy-start.9
  98.4 84.3 %copy-start.12 = (s32[1,4,1]{1,2,0:T(1,128)S(1)}, s32[1,4,1]{1,2,0:T(1,128)}, u32[]{:S(2)}) copy-start(s32[1,4,1]{1,2,0:T(1,128)} %param.15) | copy-start | bytes 52
  98.4 85.0 %copy-start.1 = (s32[1,4]{1,0:T(1,128)S(1)}, s32[1,4]{1,0:T(1,128)}, u32[]{:S(2)}) copy-start(s32[1,4]{1,0:T(1,128)} %param.16) | copy-start | bytes 52
  98.4 86.3 %copy-start.10 = (s32[1,4,128]{2,1,0:T(4,128)S(1)}, s32[1,4,128]{2,1,0:T(4,128)}, u32[]{:S(2)}) copy-start(s32[1,4,128]{2,1,0:T(4,128)} %param.17) | copy-start | bytes 6148
  102.1 5.7 %copy-start.2 = (f32[2,1024,2048]{2,1,0:T(8,128)}, f32[2,1024,2048]{2,1,0:T(8,128)S(1)}, u32[]{:S(2)}) copy-start(f32[2,1024,2048]{2,1,0:T(8,128)S(1)} %get-tuple-element.144) | copy-start | bytes 50331652 | tf_op jit(solution)/shard_map/while
  121.2 5.7 %copy-start.2 = (f32[2,1024,2048]{2,1,0:T(8,128)}, f32[2,1024,2048]{2,1,0:T(8,128)S(1)}, u32[]{:S(2)}) copy-start(f32[2,1024,2048]{2,1,0:T(8,128)S(1)} %get-tuple-element.144) | copy-start | bytes 50331652 | tf_op jit(solution)/shard_map/while
  140.2 5.7 %copy-start.2 = (f32[2,1024,2048]{2,1,0:T(8,128)}, f32[2,1024,2048]{2,1,0:T(8,128)S(1)}, u32[]{:S(2)}) copy-start(f32[2,1024,2048]{2,1,0:T(8,128)S(1)} %get-tuple-element.144) | copy-start | bytes 50331652 | tf_op jit(solution)/shard_map/while
  159.3 5.7 %copy-start.2 = (f32[2,1024,2048]{2,1,0:T(8,128)}, f32[2,1024,2048]{2,1,0:T(8,128)S(1)}, u32[]{:S(2)}) copy-start(f32[2,1024,2048]{2,1,0:T(8,128)S(1)} %get-tuple-element.144) | copy-start | bytes 50331652 | tf_op jit(solution)/shard_map/while
  174.8 39.0 %copy-start.11 = (f32[1024]{0:T(1024)S(1)}, f32[1024]{0:T(1024)}, u32[]{:S(2)}) copy-start(f32[1024]{0:T(1024)} %param.14) | copy-start | bytes 12292
  174.8 31.5 %all-to-all-start.2 = ((bf16[8,512,128]{2,1,0:T(8,128)(2,1)}), bf16[8,512,128]{2,1,0:T(8,128)(2,1)S(1)}, u32[]{:S(2)}, u32[]{:S(2)}) async-start(bf16[8,512,128]{2,1,0:T(8,128)(2,1)} %bitcast.159), calls=%async_computation.2 | async-start | bytes 2097152 | tf_op jit(solution)/shard_map/all_to_all | solution.py:93
  206.3 3.2 %copy-start.8 = (bf16[8,512,128]{2,1,0:T(8,128)(2,1)}, bf16[8,512,128]{2,1,0:T(8,128)(2,1)S(1)}, u32[]{:S(2)}) copy-start(bf16[8,512,128]{2,1,0:T(8,128)(2,1)S(1)} %all-to-all-done.2) | copy-start | bytes 3145732
  206.3 12.9 %all-to-all-start.3 = ((bf16[4,2,128]{2,1,0:T(2,128)(2,1)}), bf16[4,2,128]{2,1,0:T(2,128)(2,1)S(1)}, u32[]{:S(2)}, u32[]{:S(2)}) async-start(bf16[4,2,128]{2,1,0:T(2,128)(2,1)} %select_convert_fusion), calls=%async_computation.3 | async-start | bytes 4096 | tf_op jit(solution)/shard_map/all_to_all | solution.py:125
  212.4 1.3 copy-start.4
  219.2 30.2 %all-to-all-start.4 = ((bf16[4,2,128,1024]{3,2,1,0:T(8,128)(2,1)}), bf16[4,2,128,1024]{3,2,1,0:T(8,128)(2,1)}, u32[]{:S(2)}, u32[]{:S(2)}) async-start(bf16[4,2,128,1024]{3,2,1,0:T(8,128)(2,1)} %select_select_fusion), calls=%async_computation.4 | async-start | bytes 4194304 | tf_op jit(solution)/shard_map/all_to_all | solution.py:124
